TPU v7x, 32 devices: a whole 2x2x4 slice. The times are simulated.
32 devices in a mesh: bulk: 4 (over y, x), wide: 8 (over z, core).
Axes of the slice: x: 2, y: 2, z: 4, core: 2. Of those that a mesh axis runs over, the one named last changes fastest.
Arguments:
- particle_cell: int32 [32, 512], P(('bulk', 'wide')), may hold values from 0 to 4095
- particle_frac: float32 [32, 512], P(('bulk', 'wide')), may hold values from 0 to 1
- particle_mass: float32 [32, 512], P(('bulk', 'wide')), may hold values from 0.5 to 2
- particle_vel: float32 [3, 32, 512], P(None, ('bulk', 'wide')), may hold values from -6 to 6
- node_cell: int32 [256, 256], P(('bulk', 'wide')), may hold values from 0 to 4095
- node_body: int32 [256, 256], P(('bulk', 'wide')), may hold values from 0 to 511
- node_count: int32 [256], P(('bulk', 'wide')), may hold values from 1 to 256, as said below
- node_pos: float32 [3, 256, 256], P(None, ('bulk', 'wide')), may hold values from -4 to 4
- body_state: float32 [12, 16384], P(None, ('bulk', 'wide')), may hold values from -4 to 4, as said below
- body_vel: float32 [12, 16384], P(None, ('bulk', 'wide')), may hold values from -3 to 3
- body_mass: float32 [16384], P(('bulk', 'wide')), may hold values from 1 to 4
- touch_body: int32 [256, 128], P(('bulk', 'wide')), may hold values from 0 to 511
- touch_pos: float32 [3, 256, 128], P(None, ('bulk', 'wide')), may hold values from -4 to 4
Outputs:
- body_next: float32 [12, 16384], P(None, ('bulk', 'wide'))
- grid_velocity: float32 [3, 64, 8, 256], P(None, 'bulk', 'wide')
- touch_point: float32 [3, 256, 128], P(None, ('bulk', 'wide'))
Inputs may be any that keep to these rules, and one draw needn't show every extreme that they name: `node_count`: for each device and owner, the live node slots; every draw has an owner that receives 256 live rows from every device. `body_state`: rows 3 to 11 hold a 3 x 3 matrix within 0.3 of the identity in every entry; rows 0 to 2 within -4 to 4. `touch_body`: every device lists 128 touch slots for every owner.
All inputs are finite; a program needn't handle non-finite values.
Results may differ from a plain program's by a relative error of at most 0.0018.
Values sent between devices are 32-bit elements; how exact they have to be, the bound alone decides.
A program may use at most 64 MiB of HBM per device.

v0:
```python
import math

import jax
import jax.numpy as jnp
from jax import lax
from jax.sharding import PartitionSpec as P

LAYERS = 16
COLUMNS = 256


stiffness = 0.05
gravity_pull = -0.5


def from_behind(shard, axis, by):
    size = lax.axis_size(axis)
    pairs = [(i, i + by) for i in range(size) if 0 <= i + by < size]
    return lax.ppermute(shard, axis, pairs)


def brick_values(fractions, masses, velocities):
    lower = 1.0 - fractions
    moments = masses[None] * velocities
    stacked = jnp.concatenate(
        [
            (masses * lower)[None],
            moments * lower[None],
            (masses * fractions)[None],
            moments * fractions[None],
        ],
        axis=0,
    )
    return stacked.astype(jnp.bfloat16)


def brick_grid(operands):
    cells, fractions, masses, velocities = operands
    values = brick_values(fractions, masses, velocities)
    particles = cells.shape[0]
    block_size = math.gcd(particles, 256)
    block_count = particles // block_size
    cell_ids = lax.iota(jnp.int32, LAYERS * COLUMNS)

    def add_block(totals, item):
        block_cells, block_values = item
        table = (block_cells[:, None] == cell_ids[None, :]).astype(jnp.bfloat16)
        return (totals + jnp.dot(block_values, table, preferred_element_type=jnp.float32), None)

    items = (
        cells.reshape(block_count, block_size),
        jnp.transpose(values.reshape(8, block_count, block_size), (1, 0, 2)),
    )
    totals, unused = lax.scan(add_block, jnp.zeros((8, LAYERS * COLUMNS), jnp.float32), items)
    extended = jnp.zeros((4, (LAYERS + 1) * COLUMNS), jnp.float32)
    extended = extended.at[:, : LAYERS * COLUMNS].add(totals[:4])
    return extended.at[:, COLUMNS:].add(totals[4:])


def solve_nine(matrix, right_hand):
    matrix_rows = [matrix[number] for number in range(9)]
    right_side = [right_hand[number] for number in range(9)]
    for column in range(9):
        for lower_row in range(column + 1, 9):
            factor = matrix_rows[lower_row][column] / matrix_rows[column][column]
            matrix_rows[lower_row] = matrix_rows[lower_row] - factor * matrix_rows[column]
            right_side[lower_row] = right_side[lower_row] - factor * right_side[column]
    answer = [None] * 9
    for column in reversed(range(9)):
        residual = right_side[column]
        for column_after in range(column + 1, 9):
            residual = residual - matrix_rows[column][column_after] * answer[column_after]
        answer[column] = residual / matrix_rows[column][column]
    return jnp.stack(answer)


def newton_step(states, velocities, masses, forces):
    highest = lax.Precision.HIGHEST
    batch_size = states.shape[1]
    identity = jnp.eye(3, dtype=jnp.float32)
    affine = states[3:].reshape(3, 3, batch_size)
    moved = states[:3] + velocities[:3] + forces[:3] / masses[None]
    strain = jnp.einsum("imb,jmb->ijb", affine, affine, precision=highest) - identity[:, :, None]
    restoring = 4.0 * jnp.einsum("imb,mjb->ijb", strain, affine, precision=highest)
    gram = jnp.einsum("mlb,mjb->ljb", affine, affine, precision=highest)
    first = identity[:, None, :, None, None] * gram[None, :, None, :, :]
    second = jnp.einsum("ilb,kjb->ijklb", affine, affine, precision=highest)
    third = strain[:, None, :, None, :] * identity[None, :, None, :, None]
    hessian = 4.0 * stiffness * (first + second + third).reshape(9, 9, batch_size)
    hessian = hessian + masses[None, None] * jnp.eye(9, dtype=jnp.float32)[:, :, None]
    right_hand = (
        masses[None] * velocities[3:] + forces[3:] - stiffness * restoring.reshape(9, batch_size)
    )
    update = solve_nine(hessian, right_hand)
    return jnp.concatenate([moved, states[3:] + update], axis=0)


def place_points(picked, positions):
    affine = picked[3:].reshape((3, 3) + picked.shape[1:])
    return picked[:3] + jnp.einsum(
        "ijst,jst->ist", affine, positions, precision=lax.Precision.HIGHEST
    )


def per_device(
    particle_cell,
    particle_frac,
    particle_mass,
    particle_vel,
    node_cell,
    node_body,
    node_count,
    node_pos,
    body_state,
    body_vel,
    body_mass,
    touch_body,
    touch_pos,
):
    bricks_here = particle_cell.shape[0]
    owner_count = lax.axis_size("wide")
    body_count = body_state.shape[1]
    slot_count = node_cell.shape[1]
    bricks = lax.map(
        brick_grid, (particle_cell, particle_frac, particle_mass, jnp.moveaxis(particle_vel, 1, 0))
    )
    bricks = jnp.transpose(bricks.reshape(bricks_here, 4, LAYERS + 1, COLUMNS), (1, 2, 0, 3))
    interior = bricks[:, :LAYERS]
    ghost_layer = bricks[:, LAYERS]
    incoming = from_behind(ghost_layer, "bulk", 1)
    interior = interior.at[:, 0].add(incoming)
    mass_grid = interior[0]
    pull_vector = jnp.array([0.0, 0.0, gravity_pull], jnp.float32)
    velocity = interior[1:] / (mass_grid[None] + 1.0) + pull_vector[:, None, None, None]
    layer_ids = lax.axis_index("bulk") * LAYERS + lax.iota(jnp.int32, LAYERS)
    walls = (layer_ids == 0) | (layer_ids == lax.axis_size("bulk") * LAYERS - 1)
    velocity = jnp.where(walls[None, :, None, None], jnp.float32(0.0), velocity)
    mass_flat = mass_grid.reshape(-1)
    velocity_flat = velocity.reshape(3, -1)
    push = mass_flat[node_cell][None] * velocity_flat[:, node_cell]
    live = lax.broadcasted_iota(jnp.int32, node_cell.shape, 1) < node_count[:, None]
    push = jnp.where(live[None], push, jnp.float32(0.0))
    outer = (push[:, None] * node_pos[None]).reshape(9, owner_count, slot_count)
    general = jnp.concatenate([push, outer], axis=0)
    received, body_ids = (
        lax.all_to_all(general, "wide", split_axis=1, concat_axis=1, tiled=True),
        lax.all_to_all(node_body[None], "wide", split_axis=1, concat_axis=1, tiled=True),
    )
    forces = (
        jnp.zeros((12, body_count), jnp.float32)
        .at[:, body_ids.reshape(-1)]
        .add(received.reshape(12, -1))
    )
    body_next = newton_step(body_state, body_vel, body_mass, forces)
    looked_up = jnp.take(
        body_next,
        lax.all_to_all(touch_body, "wide", split_axis=0, concat_axis=0, tiled=True),
        axis=1,
    )
    picked = lax.all_to_all(looked_up, "wide", split_axis=1, concat_axis=1, tiled=True)
    touch_point = place_points(picked, touch_pos)
    return (body_next, velocity, touch_point)


def solution(mesh):
    placed = (
        P(("bulk", "wide"), None),
        P(("bulk", "wide"), None),
        P(("bulk", "wide"), None),
        P(None, ("bulk", "wide"), None),
        P(("bulk", "wide"), None),
        P(("bulk", "wide"), None),
        P(("bulk", "wide")),
        P(None, ("bulk", "wide"), None),
        P(None, ("bulk", "wide")),
        P(None, ("bulk", "wide")),
        P(("bulk", "wide")),
        P(("bulk", "wide"), None),
        P(None, ("bulk", "wide"), None),
    )
    return jax.shard_map(
        per_device,
        mesh=mesh,
        in_specs=placed,
        out_specs=(
            P(None, ("bulk", "wide")),
            P(None, "bulk", "wide", None),
            P(None, ("bulk", "wide"), None),
        ),
        check_vma=False,
    )
```

profile of v0, /device:TPU:0, one launch (start us, length us, event | category | flops | bytes accessed | tf_op | source)
XLA Modules:
  0.0 112.8 jit_solution(16131997454690936096)
XLA Ops:
  0.6 6.4 %all-to-all-start.2 = ((s32[8,1,128]{2,1,0:T(1,128)}), s32[8,1,128]{2,1,0:T(1,128)S(1)}, u32[]{:S(2)}, u32[]{:S(2)}) async-start(s32[8,1,128]{2,1,0:T(1,128)} %bitcast.378), calls=%async_computation.2 | async-start | bytes 8192 | tf_op jit(solution)/shard_map/all_to_all | solution.py:157
  7.0 0.6 compare_reduce_fusion
  7.6 0.5 broadcast.266
  8.1 1.3 %reduce.35 = f32[512]{0:T(512)S(1)} reduce(f32[1,512]{1,0:T(1,128)} %param.24, f32[]{:T(128)} %broadcast.266), dimensions={0}, to_apply=%param.24.reduce_sub_computation.3 | reduce | bytes 4100 | tf_op args[2]
  9.5 0.7 convert_reduce_fusion.1
  10.2 1.3 %subtract_reduce_fusion = (f32[512]{0:T(512)S(1)}, f32[512]{0:T(512)S(1)}) fusion(f32[1,512]{1,0:T(1,128)} %param.23, f32[]{:T(128)} %broadcast.266), kind=kLoop, calls=%fused_computation.273 | loop fusion | flops 512 | bytes 6148 | tf_op jit(solution)/shard_map/while/body/eval_jaxpr/sub | solution.py:23
  11.6 0.5 broadcast.268
  12.1 1.3 %reduce.36 = s32[512]{0:T(512)S(1)} reduce(s32[1,512]{1,0:T(1,128)} %param.22, s32[]{:T(128)} %broadcast.268), dimensions={0}, to_apply=%param.22.reduce_sub_computation.3 | reduce | bytes 4100 | tf_op args[0]
  13.5 0.7 reduce.16
  14.3 1.6 %while.21 = (s32[]{:T(128)}, f32[8,4096]{1,0:T(8,128)S(1)}, bf16[2,8,256]{2,1,0:T(8,128)(2,1)S(1)}, s32[2,256]{1,0:T(2,128)S(1)}, s32[]{:T(128)}, /*index=5*/s32[]{:T(128)}) while((s32[]{:T(128)}, f32[8,4096]{1,0:T(8,128)S(1)}, bf16[2,8,256]{2,1,0:T(8,128)(2,1)S(1)}, s32[2,256]{1,0:T(2,128)S(1)}, s32[]{:T(128)}, ...), condition=%wide.region_2.3_spmd.clone, body=%wide.region_1.2_spmd.clone.sunk | while | flops 17891332 | bytes 269407 | solution.py:54
  14.3 0.8 convolution_add_fusion.2
  15.2 0.8 convolution_add_fusion.2
  16.0 0.7 slice_select_fusion
  16.8 0.6 slice_bitcast_fusion.9
  17.4 4.0 %collective-permute-start = (f32[4,1,256]{2,1,0:T(1,128)}, f32[4,1,256]{2,1,0:T(1,128)}, u32[]{:S(2)}, u32[]{:S(2)}) collective-permute-start(f32[4,1,256]{2,1,0:T(1,128)} %slice_bitcast_fusion.9), channel_id=1, source_target_pairs={{0,8},{8,16},{16,24},{1,9},{9,17},{17,25},{2,10},{10,18},{18,26},{... | collective-permute-start | bytes 12296 | tf_op jit(solution)/shard_map/ppermute | solution.py:19
  21.3 0.6 fusion.21
  22.0 0.4 copy.155
  22.4 0.4 copy.161
  22.8 0.6 iota_compare_fusion.3
  23.5 3.4 %fusion.109 = f32[512,3,3]{2,1,0:T(4,128)S(1)} fusion(f32[3,3,512]{1,0,2:T(4,128)S(1)} %copy.155), kind=kOutput, calls=%fused_computation.276 | convolution fusion | flops 165888 | bytes 36864 | tf_op jit(solution)/shard_map/imb,jmb->ijb/dot_general | solution.py:83
  27.0 0.4 copy.157
  27.4 1.4 %copy.158 = f32[3,3,512]{1,0,2:T(4,128)} copy(f32[3,3,512]{2,1,0:T(4,128)S(1)} %bitcast_subtract_fusion) | data formatting | bytes 36864 | tf_op jit(solution)/shard_map/sub | solution.py:83
  28.9 4.7 %fusion.6 = f32[3,3,512]{1,0,2:T(4,128)S(1)} fusion(f32[3,3,512]{1,0,2:T(4,128)} %copy.158, f32[3,3,512]{1,0,2:T(4,128)S(1)} %copy.155), kind=kOutput, calls=%fused_computation.14 | convolution fusion | flops 170496 | bytes 55296 | tf_op jit(solution)/shard_map/imb,mjb->ijb/dot_general | solution.py:84
  33.5 4.5 %convolution_bitcast_fusion = f32[3,3,512]{0,1,2:T(4,128)} fusion(f32[3,3,512]{0,1,2:T(4,128)S(1)} %copy.161, f32[3,3,512]{1,0,2:T(4,128)S(1)} %copy.155), kind=kOutput, calls=%fused_computation.12 | convolution fusion | flops 165888 | bytes 55296 | tf_op jit(solution)/shard_map/mlb,mjb->ljb/dot_general | solution.py:85
  38.1 1.7 %copy.163 = f32[3,3,512]{2,1,0:T(4,128)S(1)} copy(f32[3,3,512]{0,1,2:T(4,128)} %convolution_bitcast_fusion) | data formatting | bytes 36864 | tf_op jit(solution)/shard_map/mlb,mjb->ljb/transpose | solution.py:85
  40.1 0.8 multiply_add_fusion
  41.2 0.4 copy-done.28
  41.9 0.4 copy-done.26
  42.4 0.6 slice_divide_fusion.3
  43.0 0.6 broadcast_in_dim.55
  44.1 0.6 mul.1186
  44.7 0.7 fusion.25
  45.4 11.8 %gather_fusion = f32[2048]{0:T(1024)S(1)} fusion(f32[4096]{0:T(1024)S(1)} %bitcast.323, s32[2048]{0:T(1024)S(1)} %broadcast_clamp_fusion), kind=kCustom, calls=%fused_computation | custom fusion | bytes 24576 | tf_op jit(solution)/shard_map/gather | solution.py:140
  57.4 0.6 copy.148
  58.0 5.5 %gather_fusion.1 = f32[2048,3]{1,0:T(8,128)S(1)} fusion(f32[3,4096]{0,1:T(8,128)S(1)} %bitcast.324, s32[2048]{0:T(1024)S(1)} %broadcast_clamp_fusion), kind=kCustom, calls=%fused_computation.1 | custom fusion | bytes 57344 | tf_op jit(solution)/shard_map/gather | solution.py:140
  63.5 0.3 copy.149
  63.9 0.7 select_bitcast_fusion.1
  64.8 0.7 copy.150
  65.5 5.1 %all-to-all-start = ((s32[1,8,256]{2,0,1:T(1,128)}), s32[1,8,256]{2,0,1:T(1,128)S(1)}, u32[]{:S(2)}, u32[]{:S(2)}) async-start(s32[1,8,256]{2,0,1:T(1,128)} %broadcast_in_dim.55), calls=%async_computation | async-start | bytes 16384 | tf_op jit(solution)/shard_map/all_to_all | solution.py:147
  70.7 5.5 %all-to-all-done = s32[1,8,256]{2,0,1:T(1,128)S(1)} async-done(((s32[1,8,256]{2,0,1:T(1,128)}), s32[1,8,256]{2,0,1:T(1,128)S(1)}, u32[]{:S(2)}, u32[]{:S(2)}) %all-to-all-start) | async-done | bytes 8224 | tf_op jit(solution)/shard_map/all_to_all | solution.py:147
  76.2 3.4 %all-to-all-start.1 = ((f32[12,8,256]{2,0,1:T(8,128)}), f32[12,8,256]{2,0,1:T(8,128)S(1)}, u32[]{:S(2)}, u32[]{:S(2)}) async-start(f32[12,8,256]{2,0,1:T(8,128)} %copy.150), calls=%async_computation.1 | async-start | bytes 262144 | tf_op jit(solution)/shard_map/all_to_all | solution.py:146
  79.6 6.7 %all-to-all-done.1 = f32[12,8,256]{2,0,1:T(8,128)S(1)} async-done(((f32[12,8,256]{2,0,1:T(8,128)}), f32[12,8,256]{2,0,1:T(8,128)S(1)}, u32[]{:S(2)}, u32[]{:S(2)}) %all-to-all-start.1) | async-done | bytes 98336 | tf_op jit(solution)/shard_map/all_to_all | solution.py:146
  86.4 0.4 copy.152
  86.8 11.5 %scatter_custom_fusion = f32[12,512]{0,1:T(8,128)S(1)} fusion(s32[2048]{0:T(1024)S(1)} %bitcast.377, f32[2048,12]{1,0:T(8,128)S(1)} %copy.152, f32[]{:T(128)} %constant.153.clone.1), kind=kCustom, calls=%fused_computation.19 | custom fusion | flops 24576 | bytes 24580 | tf_op jit(solution)/shard_map/scatter-add | solution.py:152
  99.2 1.3 %fusion.28 = (f32[1,512]{1,0:T(1,128)S(1)}, f32[1,512]{1,0:T(1,128)S(1)}, f32[1,512]{1,0:T(1,128)S(1)}, f32[1,512]{1,0:T(1,128)S(1)}, f32[1,512]{1,0:T(1,128)S(1...) fusion(f32[9,9,512]{2,1,0:T(8,128)S(1)} %multiply_add_fusion, ...), kind=kLoop, calls=%fused_computation.105 | loop fusion | flops 51200 | bytes 147456 | tf_op jit(solution)/shard_map/div | solution.py:73
  100.7 2.8 %gather_fusion.2 = f32[1024,12]{1,0:T(8,128)S(1)} fusion(f32[12,512]{0,1:T(8,128)S(1)} %copy.165, s32[1024]{0:T(1024)S(1)} %fusion.23), kind=kCustom, calls=%fused_computation.2 | custom fusion | bytes 102400 | tf_op jit(solution)/shard_map/jit(_take)/gather | solution.py:155
  103.8 8.4 %all_to_all.30 = f32[12,8,128]{2,0,1:T(8,128)S(1)} all-to-all(f32[12,8,128]{2,0,1:T(8,128)S(1)} %select_bitcast_fusion), channel_id=1, replica_groups=mesh['bulk'=4,'wide'=8] {'wide'}, dimensions={1} | all-to-all | bytes 98304 | tf_op jit(solution)/shard_map/all_to_all | solution.py:160
  112.2 0.6 copy.168
  (218 shorter events, 2.9 us)
Async XLA Ops:
  0.6 64.9 %all-to-all-start.2 = ((s32[8,1,128]{2,1,0:T(1,128)}), s32[8,1,128]{2,1,0:T(1,128)S(1)}, u32[]{:S(2)}, u32[]{:S(2)}) async-start(s32[8,1,128]{2,1,0:T(1,128)} %bitcast.378), calls=%async_computation.2 | async-start | bytes 8192 | tf_op jit(solution)/shard_map/all_to_all | solution.py:157
  14.3 7.6 %copy-start.8 = (f32[12,512]{1,0:T(8,128)S(1)}, f32[12,512]{1,0:T(8,128)}, u32[]{:S(2)}) copy-start(f32[12,512]{1,0:T(8,128)} %param.30) | copy-start | bytes 73732
  16.0 6.9 %copy-start.72 = (s32[8]{0:T(128)S(1)}, s32[8]{0:T(128)}, u32[]{:S(2)}) copy-start(s32[8]{0:T(128)} %param.28) | copy-start | bytes 100
  16.0 7.5 %copy-start.69 = (s32[8,256]{1,0:T(8,128)S(1)}, s32[8,256]{1,0:T(8,128)}, u32[]{:S(2)}) copy-start(s32[8,256]{1,0:T(8,128)} %param.26) | copy-start | bytes 24580
  17.4 27.4 %collective-permute-start = (f32[4,1,256]{2,1,0:T(1,128)}, f32[4,1,256]{2,1,0:T(1,128)}, u32[]{:S(2)}, u32[]{:S(2)}) collective-permute-start(f32[4,1,256]{2,1,0:T(1,128)} %slice_bitcast_fusion.9), channel_id=1, source_target_pairs={{0,8},{8,16},{16,24},{1,9},{9,17},{17,25},{2,10},{10,18},{18,26},{... | collective-permute-start | bytes 12296 | tf_op jit(solution)/shard_map/ppermute | solution.py:19
  33.5 6.5 %copy-start.20 = (f32[512]{0:T(512)S(1)}, f32[512]{0:T(512)}, u32[]{:S(2)}) copy-start(f32[512]{0:T(512)} %param.32) | copy-start | bytes 6148
  39.8 3.2 %copy-start.70 = (s32[8,256]{1,0:T(8,128)S(1)}, s32[8,256]{1,0:T(8,128)}, u32[]{:S(2)}) copy-start(s32[8,256]{1,0:T(8,128)} %param.27) | copy-start | bytes 24580
  41.1 2.5 %copy-start.2 = (f32[9,512]{1,0:T(8,128)}, f32[9,512]{1,0:T(8,128)S(1)}, u32[]{:S(2)}) copy-start(f32[9,512]{1,0:T(8,128)S(1)} %get-tuple-element.234) | copy-start | bytes 55300
  45.4 11.8 %copy-start.71 = (f32[3]{0:T(128)S(1)}, f32[3]{0:T(128)}, u32[]{:S(2)}) copy-start(f32[3]{0:T(128)} %constant.166.clone) | copy-start | bytes 40
  57.3 7.3 %copy-start.19 = (f32[3,8,256]{2,1,0:T(8,128)S(1)}, f32[3,8,256]{2,1,0:T(8,128)}, u32[]{:S(2)}) copy-start(f32[3,8,256]{2,1,0:T(8,128)} %param.29) | copy-start | bytes 73732
  57.4 18.8 %copy-start.3 = (f32[3,16,1,256]{3,2,1,0:T(1,128)}, f32[3,16,1,256]{3,2,1,0:T(1,128)S(1)}, u32[]{:S(2)}) copy-start(f32[3,16,1,256]{3,2,1,0:T(1,128)S(1)} %broadcast_select_fusion) | copy-start | bytes 147460
  63.8 34.9 %copy-start.9 = (f32[12,512]{1,0:T(8,128)S(1)}, f32[12,512]{1,0:T(8,128)}, u32[]{:S(2)}) copy-start(f32[12,512]{1,0:T(8,128)} %param.30) | copy-start | bytes 73732
  63.8 34.9 %copy-start.18 = (f32[12,512]{1,0:T(8,128)S(1)}, f32[12,512]{1,0:T(8,128)}, u32[]{:S(2)}) copy-start(f32[12,512]{1,0:T(8,128)} %param.31) | copy-start | bytes 73732
  64.5 34.2 %copy-start.7 = (f32[9,512]{1,0:T(8,128)S(1)}, f32[9,512]{1,0:T(8,128)}, u32[]{:S(2)}) copy-start(f32[9,512]{1,0:T(8,128)} %copy-done.6) | copy-start | bytes 55300
  64.5 34.2 %copy-start.11 = (f32[9,512]{1,0:T(8,128)S(1)}, f32[9,512]{1,0:T(8,128)}, u32[]{:S(2)}) copy-start(f32[9,512]{1,0:T(8,128)} %copy-done.10) | copy-start | bytes 55300
  64.6 34.2 %copy-start.13 = (f32[9,512]{1,0:T(8,128)S(1)}, f32[9,512]{1,0:T(8,128)}, u32[]{:S(2)}) copy-start(f32[9,512]{1,0:T(8,128)} %copy-done.12) | copy-start | bytes 55300
  64.6 34.2 %copy-start.15 = (f32[9,512]{1,0:T(8,128)S(1)}, f32[9,512]{1,0:T(8,128)}, u32[]{:S(2)}) copy-start(f32[9,512]{1,0:T(8,128)} %copy-done.14) | copy-start | bytes 55300
  64.6 34.2 %copy-start.16 = (f32[9,512]{1,0:T(8,128)S(1)}, f32[9,512]{1,0:T(8,128)}, u32[]{:S(2)}) copy-start(f32[9,512]{1,0:T(8,128)} %mul.1186) | copy-start | bytes 55300
  64.6 34.2 %copy-start.23 = (f32[1,512]{1,0:T(1,128)S(1)}, f32[1,512]{1,0:T(1,128)}, u32[]{:S(2)}) copy-start(f32[1,512]{1,0:T(1,128)} %get-tuple-element.195) | copy-start | bytes 6148
  64.6 34.2 %copy-start.36 = (f32[1,512]{1,0:T(1,128)S(1)}, f32[1,512]{1,0:T(1,128)}, u32[]{:S(2)}) copy-start(f32[1,512]{1,0:T(1,128)} %get-tuple-element.196) | copy-start | bytes 6148
  64.6 34.2 %copy-start.37 = (f32[1,512]{1,0:T(1,128)S(1)}, f32[1,512]{1,0:T(1,128)}, u32[]{:S(2)}) copy-start(f32[1,512]{1,0:T(1,128)} %get-tuple-element.197) | copy-start | bytes 6148
  64.7 34.2 %copy-start.31 = (f32[1,512]{1,0:T(1,128)S(1)}, f32[1,512]{1,0:T(1,128)}, u32[]{:S(2)}) copy-start(f32[1,512]{1,0:T(1,128)} %copy-done.30) | copy-start | bytes 6148
  64.7 34.2 %copy-start.33 = (f32[1,512]{1,0:T(1,128)S(1)}, f32[1,512]{1,0:T(1,128)}, u32[]{:S(2)}) copy-start(f32[1,512]{1,0:T(1,128)} %copy-done.32) | copy-start | bytes 6148
  64.7 34.2 %copy-start.35 = (f32[1,512]{1,0:T(1,128)S(1)}, f32[1,512]{1,0:T(1,128)}, u32[]{:S(2)}) copy-start(f32[1,512]{1,0:T(1,128)} %copy-done.34) | copy-start | bytes 6148
  64.7 34.2 %copy-start.39 = (f32[1,512]{1,0:T(1,128)S(1)}, f32[1,512]{1,0:T(1,128)}, u32[]{:S(2)}) copy-start(f32[1,512]{1,0:T(1,128)} %copy-done.38) | copy-start | bytes 6148
  64.7 34.2 %copy-start.41 = (f32[1,512]{1,0:T(1,128)S(1)}, f32[1,512]{1,0:T(1,128)}, u32[]{:S(2)}) copy-start(f32[1,512]{1,0:T(1,128)} %copy-done.40) | copy-start | bytes 6148
  64.7 34.2 %copy-start.43 = (f32[1,512]{1,0:T(1,128)S(1)}, f32[1,512]{1,0:T(1,128)}, u32[]{:S(2)}) copy-start(f32[1,512]{1,0:T(1,128)} %copy-done.42) | copy-start | bytes 6148
  64.7 34.2 %copy-start.45 = (f32[1,512]{1,0:T(1,128)S(1)}, f32[1,512]{1,0:T(1,128)}, u32[]{:S(2)}) copy-start(f32[1,512]{1,0:T(1,128)} %copy-done.44) | copy-start | bytes 6148
  64.7 34.2 %copy-start.47 = (f32[1,512]{1,0:T(1,128)S(1)}, f32[1,512]{1,0:T(1,128)}, u32[]{:S(2)}) copy-start(f32[1,512]{1,0:T(1,128)} %copy-done.46) | copy-start | bytes 6148
  64.7 34.2 %copy-start.49 = (f32[1,512]{1,0:T(1,128)S(1)}, f32[1,512]{1,0:T(1,128)}, u32[]{:S(2)}) copy-start(f32[1,512]{1,0:T(1,128)} %copy-done.48) | copy-start | bytes 6148
  64.7 34.2 %copy-start.51 = (f32[1,512]{1,0:T(1,128)S(1)}, f32[1,512]{1,0:T(1,128)}, u32[]{:S(2)}) copy-start(f32[1,512]{1,0:T(1,128)} %copy-done.50) | copy-start | bytes 6148
  64.8 34.2 %copy-start.53 = (f32[1,512]{1,0:T(1,128)S(1)}, f32[1,512]{1,0:T(1,128)}, u32[]{:S(2)}) copy-start(f32[1,512]{1,0:T(1,128)} %copy-done.52) | copy-start | bytes 6148
  64.8 34.2 %copy-start.55 = (f32[1,512]{1,0:T(1,128)S(1)}, f32[1,512]{1,0:T(1,128)}, u32[]{:S(2)}) copy-start(f32[1,512]{1,0:T(1,128)} %copy-done.54) | copy-start | bytes 6148
  64.8 34.2 %copy-start.57 = (f32[1,512]{1,0:T(1,128)S(1)}, f32[1,512]{1,0:T(1,128)}, u32[]{:S(2)}) copy-start(f32[1,512]{1,0:T(1,128)} %copy-done.56) | copy-start | bytes 6148
  64.8 34.2 %copy-start.59 = (f32[1,512]{1,0:T(1,128)S(1)}, f32[1,512]{1,0:T(1,128)}, u32[]{:S(2)}) copy-start(f32[1,512]{1,0:T(1,128)} %copy-done.58) | copy-start | bytes 6148
  64.8 34.2 %copy-start.61 = (f32[1,512]{1,0:T(1,128)S(1)}, f32[1,512]{1,0:T(1,128)}, u32[]{:S(2)}) copy-start(f32[1,512]{1,0:T(1,128)} %copy-done.60) | copy-start | bytes 6148
  64.8 34.2 %copy-start.63 = (f32[1,512]{1,0:T(1,128)S(1)}, f32[1,512]{1,0:T(1,128)}, u32[]{:S(2)}) copy-start(f32[1,512]{1,0:T(1,128)} %copy-done.62) | copy-start | bytes 6148
  64.8 34.2 %copy-start.65 = (f32[1,512]{1,0:T(1,128)S(1)}, f32[1,512]{1,0:T(1,128)}, u32[]{:S(2)}) copy-start(f32[1,512]{1,0:T(1,128)} %copy-done.64) | copy-start | bytes 6148
  64.8 34.2 %copy-start.67 = (f32[1,512]{1,0:T(1,128)S(1)}, f32[1,512]{1,0:T(1,128)}, u32[]{:S(2)}) copy-start(f32[1,512]{1,0:T(1,128)} %copy-done.66) | copy-start | bytes 6148
  65.5 10.7 %all-to-all-start = ((s32[1,8,256]{2,0,1:T(1,128)}), s32[1,8,256]{2,0,1:T(1,128)S(1)}, u32[]{:S(2)}, u32[]{:S(2)}) async-start(s32[1,8,256]{2,0,1:T(1,128)} %broadcast_in_dim.55), calls=%async_computation | async-start | bytes 16384 | tf_op jit(solution)/shard_map/all_to_all | solution.py:147
  70.7 28.5 %copy-start.1 = (f32[9,512]{1,0:T(8,128)S(1)}, f32[9,512]{1,0:T(8,128)}, u32[]{:S(2)}) copy-start(f32[9,512]{1,0:T(8,128)} %copy-done) | copy-start | bytes 55300
  70.7 28.5 %copy-start.22 = (f32[1,512]{1,0:T(1,128)S(1)}, f32[1,512]{1,0:T(1,128)}, u32[]{:S(2)}) copy-start(f32[1,512]{1,0:T(1,128)} %copy-done.21) | copy-start | bytes 6148
  70.7 28.5 %copy-start.25 = (f32[1,512]{1,0:T(1,128)S(1)}, f32[1,512]{1,0:T(1,128)}, u32[]{:S(2)}) copy-start(f32[1,512]{1,0:T(1,128)} %copy-done.24) | copy-start | bytes 6148
  70.7 28.5 %copy-start.27 = (f32[1,512]{1,0:T(1,128)S(1)}, f32[1,512]{1,0:T(1,128)}, u32[]{:S(2)}) copy-start(f32[1,512]{1,0:T(1,128)} %copy-done.26) | copy-start | bytes 6148
  70.7 28.5 %copy-start.29 = (f32[1,512]{1,0:T(1,128)S(1)}, f32[1,512]{1,0:T(1,128)}, u32[]{:S(2)}) copy-start(f32[1,512]{1,0:T(1,128)} %copy-done.28) | copy-start | bytes 6148
  76.2 10.1 %all-to-all-start.1 = ((f32[12,8,256]{2,0,1:T(8,128)}), f32[12,8,256]{2,0,1:T(8,128)S(1)}, u32[]{:S(2)}, u32[]{:S(2)}) async-start(f32[12,8,256]{2,0,1:T(8,128)} %copy.150), calls=%async_computation.1 | async-start | bytes 262144 | tf_op jit(solution)/shard_map/all_to_all | solution.py:146
  86.8 25.4 %copy-start.68 = (f32[3,8,128]{2,1,0:T(8,128)S(1)}, f32[3,8,128]{2,1,0:T(8,128)}, u32[]{:S(2)}) copy-start(f32[3,8,128]{2,1,0:T(8,128)} %param.34) | copy-start | bytes 36868
  100.6 12.3 %copy-start.17 = (f32[12,512]{1,0:T(8,128)}, f32[12,512]{1,0:T(8,128)S(1)}, u32[]{:S(2)}) copy-start(f32[12,512]{1,0:T(8,128)S(1)} %pad_maximum_fusion.1) | copy-start | bytes 73732
  (29 other events, 29.1 us)
where the time goes:
time: 114 us; the launch traced here: 113 us
  local copies, waits for them, and re-layouts  32.5 us (29%)
  other arithmetic  24.6 us (22%)
  starting transfers between devices  18.8 us (16%)
  matrix products  14.2 us (12%)
  waiting for transfers between devices  12.2 us (11%)
  blocking collectives  8.4 us (7%)
  between operations  2.03 us (2%)
    gather x4, local copies, waits for them, and re-layouts, per_device(): push = mass_flat[node_cell][None] * velocity_flat[:, node_cell]  17.6 us
    scatter-add x1, other arithmetic, per_device(): forces = jnp.zeros((12, body_count), jnp.float32).at[:, body_ids.reshape(...  11.5 us
    all_to_all x1, blocking collectives, per_device(): lax.all_to_all(looked_up, 'wide', split_axis=1, concat_axis=1, tiled=True)  8.4 us
    all_to_all x1, waiting for transfers between devices, per_device(): lax.all_to_all(general, 'wide', split_axis=1, concat_axis=1, tiled=True)  6.67 us
    all_to_all x1, starting transfers between devices, per_device(): lax.all_to_all(touch_body, 'wide', split_axis=0, concat_axis=0, tiled=True)  6.37 us
    all_to_all x1, waiting for transfers between devices, per_device(): lax.all_to_all(node_body[None], 'wide', split_axis=1, concat_axis=1, tile...  5.54 us
    all_to_all x1, starting transfers between devices, per_device(): lax.all_to_all(node_body[None], 'wide', split_axis=1, concat_axis=1, tile...  5.11 us
    dot_general x1, matrix products, newton_step(): jnp.einsum('imb,mjb->ijb', strain, affine, precision=highest)  4.68 us
  transfers between devices with their start and end apart: 4, of which 2 were waited for; matrix products, arithmetic and copies ran while one was open for 47% of the time, Pallas kernels for 0%

commit v1 on v0

v1 whole, which is shorter than its diff:
```python
import functools

import jax
import jax.numpy as jnp
from jax import lax
from jax.experimental import pallas as pl
from jax.experimental.pallas import tpu as pltpu
from jax.sharding import PartitionSpec as P

LAYERS = 16
COLUMNS = 256
LANES = 128
MESH = pl.DeviceIdType.MESH

stiffness = 0.05
gravity_pull = -0.5


def split_parts(value):
    coarse = value.astype(jnp.bfloat16).astype(jnp.float32)
    return coarse, value - coarse


def one_hot(ids, rows):
    found = lax.broadcasted_iota(jnp.int32, (rows, ids.shape[1]), 0) == ids
    return jnp.where(found, 1.0, 0.0).astype(jnp.bfloat16)


def dot_nt(left, right):
    return lax.dot_general(
        left, right, (((1,), (1,)), ((), ())), preferred_element_type=jnp.float32
    )


def particle_sums(cells, fractions, masses, velocities):
    particles = cells.shape[1]
    layer, column = cells // COLUMNS, cells % COLUMNS
    below = 1.0 - fractions
    moments = [masses] + [masses * velocities[axis] for axis in range(3)]
    lower = [moment * below for moment in moments]
    upper = [moment * fractions for moment in moments]
    layer_ids = lax.broadcasted_iota(jnp.int32, (LAYERS, particles), 0)
    here, next_up = layer_ids == layer, layer_ids == layer + 1
    rows = [
        jnp.where(here, low, jnp.where(next_up, high, 0.0)) for low, high in zip(lower, upper)
    ]
    channel_ids = lax.broadcasted_iota(jnp.int32, (8, particles), 0)
    past = jnp.zeros((8, particles), jnp.float32)
    for channel in range(4):
        past = jnp.where(channel_ids == channel, upper[channel], past)
    past = jnp.where(layer == LAYERS - 1, past, 0.0)
    table = jnp.concatenate(rows + [past], axis=0).astype(jnp.bfloat16)
    return dot_nt(table, one_hot(column, COLUMNS))


def factorise(affine, masses):
    strain, gram = {}, {}
    for i in range(3):
        for j in range(i, 3):
            strain[i, j] = sum(affine[i][m] * affine[j][m] for m in range(3))
            if i == j:
                strain[i, j] = strain[i, j] - 1.0
            gram[i, j] = sum(affine[m][i] * affine[m][j] for m in range(3))
            strain[j, i], gram[j, i] = strain[i, j], gram[i, j]
    matrix = {}
    for row in range(9):
        i, j = divmod(row, 3)
        for other in range(row, 9):
            k, l = divmod(other, 3)
            entry = affine[i][l] * affine[k][j]
            if i == k:
                entry = entry + gram[l, j]
            if j == l:
                entry = entry + strain[i, k]
            entry = (4.0 * stiffness) * entry
            if row == other:
                entry = entry + masses
            matrix[row, other] = entry
    factors, inverses = {}, []
    for column in range(9):
        inverse = 1.0 / matrix[column, column]
        inverses.append(inverse)
        for row in range(column + 1, 9):
            factors[row, column] = matrix[column, row] * inverse
        for row in range(column + 1, 9):
            for other in range(row, 9):
                matrix[row, other] = (
                    matrix[row, other] - factors[row, column] * matrix[column, other]
                )
    restoring = [
        4.0 * sum(strain[i, m] * affine[m][j] for m in range(3))
        for i in range(3)
        for j in range(3)
    ]
    return factors, inverses, restoring


def kernel(
    bulk_size,
    wide_size,
    cell_ref,
    frac_ref,
    pmass_ref,
    pvel_ref,
    node_cell_ref,
    node_body_ref,
    count_ref,
    node_pos_ref,
    state_ref,
    bvel_ref,
    bmass_ref,
    touch_body_ref,
    touch_pos_ref,
    next_ref,
    grid_ref,
    point_ref,
    ghost_out,
    ghost_in,
    body_in,
    pos_in,
    tbody_in,
    tpos_in,
    push_out,
    push_in,
    point_out,
    point_in,
    states,
    speeds,
    weights,
    solver,
    node_hot,
    body_hot,
    touch_hot,
    send_sem,
    recv_sem,
    ghost_sem,
):
    bulk, wide = lax.axis_index("bulk"), lax.axis_index("wide")
    slots = node_cell_ref.shape[1]
    touches = touch_body_ref.shape[1]
    heads = state_ref.shape[1] // LANES
    pieces = 2 * heads
    following = lax.rem(bulk + 1, bulk_size)
    previous = lax.rem(bulk + bulk_size - 1, bulk_size)
    peers = [lax.rem(wide + step, wide_size) for step in range(1, wide_size)]

    barrier = pltpu.get_barrier_semaphore()
    for peer in peers:
        pl.semaphore_signal(barrier, inc=1, device_id=(bulk, peer), device_id_type=MESH)
    for other in (following, previous):
        pl.semaphore_signal(barrier, inc=1, device_id=(other, wide), device_id_type=MESH)

    sums = particle_sums(
        cell_ref[...], frac_ref[...], pmass_ref[...], [pvel_ref[axis] for axis in range(3)]
    )
    ghost_out[...] = sums[4 * LAYERS :]

    pl.semaphore_wait(barrier, wide_size + 1)

    ghost = pltpu.make_async_remote_copy(
        src_ref=ghost_out,
        dst_ref=ghost_in,
        send_sem=ghost_sem.at[0],
        recv_sem=ghost_sem.at[1],
        device_id=(following, wide),
        device_id_type=MESH,
    )
    ghost.start()

    def exchange(kind, source, target, is_row):
        def pick(ref, index):
            row = pl.ds(index, 1)
            return ref.at[row, :] if is_row else ref.at[:, row, :]

        sends = []
        for number, peer in enumerate(peers):
            sends.append(
                pltpu.make_async_remote_copy(
                    src_ref=pick(source, peer),
                    dst_ref=pick(target, wide),
                    send_sem=send_sem.at[kind, number],
                    recv_sem=recv_sem.at[kind, wide],
                    device_id=(bulk, peer),
                    device_id_type=MESH,
                )
            )
            sends[-1].start()
        if is_row:
            target[pl.ds(wide, 1), :] = source[pl.ds(wide, 1), :]
        else:
            target[:, pl.ds(wide, 1), :] = source[:, pl.ds(wide, 1), :]

        def arrive():
            for number, peer in enumerate(peers):
                pltpu.make_async_remote_copy(
                    src_ref=pick(source, peer),
                    dst_ref=pick(target, peer),
                    send_sem=send_sem.at[kind, number],
                    recv_sem=recv_sem.at[kind, peer],
                    device_id=(bulk, peer),
                    device_id_type=MESH,
                ).wait_recv()

        def leave():
            for send in sends:
                send.wait_send()

        return arrive, leave

    early = [
        exchange(0, node_body_ref, body_in, True),
        exchange(1, touch_body_ref, tbody_in, True),
        exchange(2, node_pos_ref, pos_in, False),
        exchange(3, touch_pos_ref, tpos_in, False),
    ]

    for owner in range(wide_size):
        node_hot[owner] = one_hot(node_cell_ref[owner : owner + 1, :] % COLUMNS, COLUMNS)

    for channel in range(12):
        for head in range(heads):
            lanes = slice(head * LANES, (head + 1) * LANES)
            for copy in range(2):
                place = slice(copy * heads + head, copy * heads + head + 1)
                states[channel, place, :] = state_ref[channel : channel + 1, lanes]
                speeds[channel, place, :] = bvel_ref[channel : channel + 1, lanes]
    for head in range(heads):
        for copy in range(2):
            place = slice(copy * heads + head, copy * heads + head + 1)
            weights[place, :] = bmass_ref[head : head + 1, :]

    ghost.wait()
    layer_ids = lax.broadcasted_iota(jnp.int32, (LAYERS, COLUMNS), 0)
    keep = jnp.logical_and(layer_ids == 0, bulk > 0)
    grid = [
        sums[channel * LAYERS : (channel + 1) * LAYERS]
        + jnp.where(keep, ghost_in[channel : channel + 1, :], 0.0)
        for channel in range(4)
    ]
    whole_ids = layer_ids + bulk * LAYERS
    walls = jnp.logical_or(whole_ids == 0, whole_ids == bulk_size * LAYERS - 1)
    tables = []
    velocities = []
    for axis in range(3):
        velocity = grid[axis + 1] / (grid[0] + 1.0)
        if axis == 2:
            velocity = velocity + gravity_pull
        velocity = jnp.where(walls, 0.0, velocity)
        velocities.append(velocity)
        tables.extend(split_parts(grid[0] * velocity))
    table = jnp.concatenate(tables, axis=0).astype(jnp.bfloat16)

    node_layers = lax.broadcasted_iota(jnp.int32, (LAYERS, slots), 0)
    slot_ids = lax.broadcasted_iota(jnp.int32, (1, slots), 1)
    for owner in range(wide_size):
        found = jnp.dot(table, node_hot[owner], preferred_element_type=jnp.float32)
        chosen = node_layers == node_cell_ref[owner : owner + 1, :] // COLUMNS
        live = slot_ids < count_ref[owner]
        for axis in range(3):
            start = 2 * LAYERS * axis
            both = found[start : start + LAYERS] + found[start + LAYERS : start + 2 * LAYERS]
            push = jnp.sum(jnp.where(chosen, both, 0.0), axis=0, keepdims=True)
            push_out[axis, owner : owner + 1, :] = jnp.where(live, push, 0.0)

    push_arrive, push_leave = exchange(4, push_out, push_in, False)

    for axis in range(3):
        grid_ref[axis] = velocities[axis]

    affine = [[states[3 + 3 * i + j] for j in range(3)] for i in range(3)]
    weight = weights[...]
    factors, inverses, restoring = factorise(affine, weight)
    names = {}
    for name, value in (
        [(key, value) for key, value in factors.items()]
        + [(("inverse", number), value) for number, value in enumerate(inverses)]
        + [
            (("right", number), weight * speeds[3 + number] - stiffness * restoring[number])
            for number in range(9)
        ]
        + [(("moved", number), states[number] + speeds[number]) for number in range(3)]
        + [(("lightness", 0), 1.0 / weight)]
    ):
        names[name] = len(names)
        solver[names[name]] = value

    for arrive, leave in early:
        arrive()
    piece_ids = lax.broadcasted_iota(jnp.int32, (pieces, slots), 0)
    for source in range(wide_size):
        body_hot[source] = one_hot(body_in[source : source + 1, :] % LANES, LANES)
        touch_hot[:, source * touches : (source + 1) * touches] = one_hot(
            tbody_in[source : source + 1, :] % LANES, LANES
        )

    push_arrive()
    force = [push_in[axis] for axis in range(3)]
    arm = [pos_in[axis] for axis in range(3)]
    general = force + [force[i] * arm[j] for i in range(3) for j in range(3)]
    totals = jnp.zeros((12 * pieces, LANES), jnp.float32)
    for source in range(wide_size):
        chosen = piece_ids % heads == body_in[source : source + 1, :] // LANES
        rows = []
        for value in general:
            coarse, rest = split_parts(value[source : source + 1, :])
            rows.append(jnp.where(chosen, jnp.where(piece_ids < heads, coarse, rest), 0.0))
        left = jnp.concatenate(rows, axis=0).astype(jnp.bfloat16)
        totals = totals + dot_nt(left, body_hot[source])

    sums_of = []
    for channel in range(12):
        total = totals[channel * pieces : (channel + 1) * pieces]
        sums_of.append(total + pltpu.roll(total, heads, 0))
    following_state = [
        solver[names["moved", number]] + sums_of[number] * solver[names["lightness", 0]]
        for number in range(3)
    ]
    answer = [solver[names["right", number]] + sums_of[3 + number] for number in range(9)]
    for column in range(9):
        for row in range(column + 1, 9):
            answer[row] = answer[row] - solver[names[row, column]] * answer[column]
    for column in range(9):
        answer[column] = answer[column] * solver[names["inverse", column]]
    for column in reversed(range(9)):
        for row in range(column):
            answer[row] = answer[row] - solver[names[column, row]] * answer[column]
    following_state += [states[3 + number] + answer[number] for number in range(9)]

    first_half = lax.broadcasted_iota(jnp.int32, (pieces, LANES), 0) < heads
    body_table = jnp.concatenate(
        [jnp.where(first_half, *split_parts(value)) for value in following_state], axis=0
    ).astype(jnp.bfloat16)
    looked_up = jnp.dot(body_table, touch_hot[...], preferred_element_type=jnp.float32)
    touch_pieces = lax.broadcasted_iota(jnp.int32, (pieces, touches), 0) % heads
    for source in range(wide_size):
        chosen = touch_pieces == tbody_in[source : source + 1, :] // LANES
        lanes = slice(source * touches, (source + 1) * touches)
        place = [tpos_in[axis, source : source + 1, :] for axis in range(3)]

        def part(channel):
            return looked_up[channel * pieces : (channel + 1) * pieces, lanes]

        for i in range(3):
            point = part(i)
            for j in range(3):
                point = point + part(3 + 3 * i + j) * place[j]
            point_out[i, source : source + 1, :] = jnp.sum(
                jnp.where(chosen, point, 0.0), axis=0, keepdims=True
            )

    point_arrive, point_leave = exchange(5, point_out, point_in, False)

    for channel in range(12):
        for head in range(heads):
            lanes = slice(head * LANES, (head + 1) * LANES)
            next_ref[channel : channel + 1, lanes] = following_state[channel][head : head + 1, :]

    for arrive, leave in early:
        leave()
    push_leave()
    point_leave()
    point_arrive()
    point_ref[...] = point_in[...]


def per_device(
    particle_cell,
    particle_frac,
    particle_mass,
    particle_vel,
    node_cell,
    node_body,
    node_count,
    node_pos,
    body_state,
    body_vel,
    body_mass,
    touch_body,
    touch_pos,
):
    bulk_size, wide_size = lax.axis_size("bulk"), lax.axis_size("wide")
    body_count = body_state.shape[1]
    slots, touches = node_cell.shape[1], touch_body.shape[1]
    pieces = 2 * (body_count // LANES)
    vmem = pl.BlockSpec(memory_space=pltpu.VMEM)
    smem = pl.BlockSpec(memory_space=pltpu.SMEM)
    f32, i32, bf16 = jnp.float32, jnp.int32, jnp.bfloat16
    body_next, velocity, touch_point = pl.pallas_call(
        functools.partial(kernel, bulk_size, wide_size),
        name="substep",
        out_shape=(
            jax.ShapeDtypeStruct(body_state.shape, f32),
            jax.ShapeDtypeStruct((3, LAYERS, COLUMNS), f32),
            jax.ShapeDtypeStruct(touch_pos.shape, f32),
        ),
        in_specs=[vmem] * 6 + [smem] + [vmem] * 6,
        out_specs=(vmem, vmem, vmem),
        scratch_shapes=[
            pltpu.VMEM((8, COLUMNS), f32),
            pltpu.VMEM((8, COLUMNS), f32),
            pltpu.VMEM((wide_size, slots), i32),
            pltpu.VMEM((3, wide_size, slots), f32),
            pltpu.VMEM((wide_size, touches), i32),
            pltpu.VMEM((3, wide_size, touches), f32),
            pltpu.VMEM((3, wide_size, slots), f32),
            pltpu.VMEM((3, wide_size, slots), f32),
            pltpu.VMEM((3, wide_size, touches), f32),
            pltpu.VMEM((3, wide_size, touches), f32),
            pltpu.VMEM((12, pieces, LANES), f32),
            pltpu.VMEM((12, pieces, LANES), f32),
            pltpu.VMEM((pieces, LANES), f32),
            pltpu.VMEM((58, pieces, LANES), f32),
            pltpu.VMEM((wide_size, COLUMNS, slots), bf16),
            pltpu.VMEM((wide_size, LANES, slots), bf16),
            pltpu.VMEM((LANES, wide_size * touches), bf16),
            pltpu.SemaphoreType.DMA((6, wide_size)),
            pltpu.SemaphoreType.DMA((6, wide_size)),
            pltpu.SemaphoreType.DMA((2,)),
        ],
        compiler_params=pltpu.CompilerParams(collective_id=0, has_side_effects=True),
    )(
        particle_cell,
        particle_frac,
        particle_mass,
        particle_vel,
        node_cell,
        node_body,
        node_count,
        node_pos,
        body_state,
        body_vel,
        body_mass.reshape(-1, LANES),
        touch_body,
        touch_pos,
    )
    return body_next, velocity[:, :, None, :], touch_point


def solution(mesh):
    split = ("bulk", "wide")
    placed = (
        P(split, None),
        P(split, None),
        P(split, None),
        P(None, split, None),
        P(split, None),
        P(split, None),
        P(split),
        P(None, split, None),
        P(None, split),
        P(None, split),
        P(split),
        P(split, None),
        P(None, split, None),
    )
    return jax.shard_map(
        per_device,
        mesh=mesh,
        in_specs=placed,
        out_specs=(
            P(None, split),
            P(None, "bulk", "wide", None),
            P(None, split, None),
        ),
        check_vma=False,
    )
```

time: 114 us -> 23.5 us (0.21)
  local copies, waits for them, and re-layouts: 32.5 us -> 2.8 us
  other arithmetic: 24.6 us -> 0 us
  Pallas kernels: 0 us -> 19.7 us
  starting transfers between devices: 18.8 us -> 0 us
  matrix products: 14.2 us -> 0 us
  waiting for transfers between devices: 12.2 us -> 0 us
  blocking collectives: 8.4 us -> 0 us
  between operations: 2.03 us -> 0.65 us
    gather x6 -> x0, local copies, waits for them, and re-layouts: 20.6 us -> none  [the longest x4 17.6 us: per_device(): push = mass_flat[node_cell][None] * velocity_flat[:, node_cell]]
    pallas_call x0 -> x1, Pallas kernels: none -> 19.7 us  [per_device(): pl.pallas_call(functools.partial(kernel, bulk_size, wide_size), name='sub...]
    all_to_all x3 -> x0, starting transfers between devices: 14.8 us -> none  [the longest x1 6.37 us: per_device(): lax.all_to_all(touch_body, 'wide', split_axis=0, concat_axis=0, tiled=True)]
    dot_general x5 -> x0, matrix products: 14.2 us -> none  [the longest x1 4.68 us: newton_step(): jnp.einsum('imb,mjb->ijb', strain, affine, precision=highest)]
    scatter-add x3 -> x0, other arithmetic: 12.3 us -> none  [the longest x1 11.5 us: per_device(): forces = jnp.zeros((12, body_count), jnp.float32).at[:, body_ids.reshape(...]
    all_to_all x3 -> x0, waiting for transfers between devices: 12.2 us -> none  [the longest x1 6.67 us: per_device(): lax.all_to_all(general, 'wide', split_axis=1, concat_axis=1, tiled=True)]
    all_to_all x1 -> x0, blocking collectives: 8.4 us -> none  [per_device(): lax.all_to_all(looked_up, 'wide', split_axis=1, concat_axis=1, tiled=True)]
    ppermute x1 -> x0, starting transfers between devices: 3.98 us -> none  [from_behind(): return lax.ppermute(shard, axis, pairs)]
  transfers between devices with their start and end apart: 4 -> 0, of which waited for: 2 -> 0; matrix products, arithmetic and copies ran while one was open for 47% -> 0% of each run, Pallas kernels for 0% -> 0%
where the time goes in v1:
time: 23.5 us; the launch traced here: 23.2 us
  Pallas kernels  19.7 us (84%)
  local copies, waits for them, and re-layouts  2.8 us (12%)
  between operations  0.65 us (3%)
    pallas_call x1, Pallas kernels, per_device(): pl.pallas_call(functools.partial(kernel, bulk_size, wide_size), name='sub...  19.7 us
    unnamed x7, local copies, waits for them, and re-layouts  2.8 us

profile of v1, /device:TPU:0, one launch (start us, length us, event | category | flops | bytes accessed | tf_op | source)
XLA Modules:
  0.0 23.2 jit_solution(9120273290627216258)
XLA Ops:
  0.6 19.7 %substep.1 = (f32[12,512]{1,0:T(8,128)}, f32[3,16,256]{2,1,0:T(8,128)}, f32[3,8,128]{2,1,0:T(8,128)}) custom-call(s32[1,512]{1,0:T(1,128)} %cell_ref.1, f32[1,512]{1,0:T(1,128)} %frac_ref.1, f32[1,512]{1,0:T(1,128)} %pmass_ref.1, f32[3,1,512]{2,1,0:T(1,128)} %pvel_ref.1, s32[8,256]{1,0:T(8,128)} %node_cell_ref.1, s32[8,256]{1,0:T(8,128)} %node_body_ref.1, ...), custom_call_target="tpu_custom_call" | custom-call | tf_op jit(solution)/shard_map/substep/pallas_call | solution.py:388
  20.4 0.0 copy-start
  20.4 1.5 %copy.16 = f32[3,16,1,256]{3,2,1,0:T(1,128)} copy(f32[3,16,1,256]{3,1,0,2:T(8,128)} %bitcast.2) | data formatting | bytes 98304
  21.9 0.0 copy-done
  21.9 0.0 copy-start.1
  21.9 0.6 %copy.19 = f32[12,512]{1,0:T(8,128)} copy(f32[12,512]{1,0:T(8,128)S(1)} %copy-done) | data formatting | bytes 49152
  22.5 0.1 copy-done.1
  22.6 0.6 %copy.20 = f32[3,8,128]{2,1,0:T(8,128)} copy(f32[3,8,128]{2,1,0:T(8,128)S(1)} %copy-done.1) | data formatting | bytes 24576
Async XLA Ops:
  20.4 1.5 %copy-start = (f32[12,512]{1,0:T(8,128)S(1)}, f32[12,512]{1,0:T(8,128)}, u32[]{:S(2)}) copy-start(f32[12,512]{1,0:T(8,128)} %get-tuple-element.15) | copy-start | bytes 73732
  21.9 0.7 %copy-start.1 = (f32[3,8,128]{2,1,0:T(8,128)S(1)}, f32[3,8,128]{2,1,0:T(8,128)}, u32[]{:S(2)}) copy-start(f32[3,8,128]{2,1,0:T(8,128)} %get-tuple-element.17) | copy-start | bytes 36868
